TPU v7x, 32 devices: a whole 2x2x4 slice. The times are simulated.
32 devices in a mesh: sec: 4 (over y, x), gx: 8 (over z, core).
Axes of the slice: x: 2, y: 2, z: 4, core: 2. Of those that a mesh axis runs over, the one named last changes fastest.
Arguments:
- pressure_start: float32 [16, 128, 1024], P('sec', 'gx'), may hold values from -8 to 8
- soil_type: int32 [16, 128, 1024], P('sec', 'gx'), may hold values from 0 to 11
- saturated_conductivity: float32 [12], replicated, may hold values from 0.2 to 5
- storage_coefficient: float32 [12], replicated, may hold values from 0.1 to 1
- rainfall: float32 [3, 128, 1024], P(None, 'gx'), may hold values from 0 to 2
Outputs:
- pressure: float32 [16, 128, 1024], P('sec', 'gx')
- inflow: float32 [4, 3, 128, 1024], P('sec', None, 'gx')
All inputs are finite; a program needn't handle non-finite values.
Results may differ from a plain program's by a relative error of at most 0.0001.
Values sent between devices are 32-bit elements; how exact they have to be, the bound alone decides.
A program may use at most 64 MiB of HBM per device.

v0:
```python
import jax
import jax.numpy as jnp
from jax import lax
from jax.sharding import PartitionSpec as P

ITERS = 4


def prefix(shard, axis, combine, identity, reverse):
    count, here = (lax.axis_size(axis), lax.axis_index(axis))
    everything = jax.tree.map(lambda part: lax.all_gather(part, axis), shard)
    start = jax.tree.map(
        lambda part, zero: jnp.broadcast_to(jnp.asarray(zero, part.dtype), part.shape),
        shard,
        identity,
    )

    def lap(k, before):
        at = count - 1 - k if reverse else k
        reached = at > here if reverse else at < here
        new = combine(before, jax.tree.map(lambda part: part[at], everything))
        return jax.tree.map(lambda a, b: jnp.where(reached, a, b), new, before)

    return lax.fori_loop(0, count, lap, start)


def padded_2(block, sides, width):
    for axis, dim in sides:
        count = lax.axis_size(axis)
        forward = [(i, i + 1) for i in range(count - 1)]
        backward = [(target, source) for source, target in forward]
        low = lax.ppermute(
            lax.slice_in_dim(block, block.shape[dim] - width, None, axis=dim), axis, forward
        )
        high = lax.ppermute(lax.slice_in_dim(block, 0, width, axis=dim), axis, backward)
        block = jnp.concatenate([low, block, high], axis=dim)
    return block


def lookup(kinds, table):
    total = jnp.zeros(kinds.shape, jnp.float32)
    for kind in range(table.shape[0]):
        total = jnp.where(kinds == kind, table[kind], total)
    return total


def harmonic(cond, other):
    return 2.0 * cond * other / (cond + other)


def neighbours(padded):
    return [
        padded[:-2, 1:-1, 1:-1],
        padded[2:, 1:-1, 1:-1],
        padded[1:-1, :-2, 1:-1],
        padded[1:-1, 2:, 1:-1],
        padded[1:-1, 1:-1, :-2],
        padded[1:-1, 1:-1, 2:],
    ]


def pad_side(rimmed):
    return jnp.pad(rimmed, ((0, 0), (0, 0), (1, 1)))


def face_terms(conductivity, padded):
    return [harmonic(conductivity, other) for other in neighbours(padded)]


def stencil(field, padded, faces, capacity):
    result = capacity * field
    for face, other in zip(faces, neighbours(padded)):
        result = result + face * (field - other)
    return result


def affine(earlier, later):
    return (earlier[0] * later[0], later[0] * earlier[1] + later[1])


def adding(earlier, later):
    return earlier + later


def body(pressure_start, soil_type, saturated_conductivity, storage_coefficient, rainfall):
    cond_table = lookup(soil_type, saturated_conductivity)
    store_table = lookup(soil_type, storage_coefficient)
    head = pressure_start
    layers = head.shape[0]
    depth = jnp.float32(layers)
    flows = []
    for step in range(rainfall.shape[0]):
        saturation = jax.nn.sigmoid(head)
        conductivity = cond_table * (0.05 + saturation * saturation)
        capacity = store_table * (0.1 + saturation * (1.0 - saturation))
        water = jnp.sum(saturation, axis=0)
        bottom = conductivity[layers - 1]
        ones_field = jnp.ones_like(water)
        zero_field = jnp.zeros_like(water)
        below = prefix(water, "sec", adding, zero_field, True)
        slope = water / depth * (0.5 + 0.5 * below / (below + depth))
        offset = 0.5 * bottom
        prefix_a, prefix_b = prefix((slope, offset), "sec", affine, (ones_field, zero_field), False)
        entering = prefix_a * rainfall[step] + prefix_b
        leaving = slope * entering + offset
        flows.append(entering)
        source = jnp.zeros(head.shape, jnp.float32).at[0].add(entering).at[layers - 1].add(-leaving)

        def apply(field):
            paired = jnp.stack([field, conductivity])
            rimmed = padded_2(paired, (("sec", 1), ("gx", 2)), 1)
            faces_now = face_terms(conductivity, pad_side(rimmed[1]))
            return (stencil(field, pad_side(rimmed[0]), faces_now, capacity), faces_now)

        start_image, faces = apply(head)
        gravity = faces[0] - faces[1]
        rhs = capacity * head + gravity + source
        diagonal = capacity
        for face in faces:
            diagonal = diagonal + face
        iterate = head
        residual = rhs - start_image
        direction = residual
        along = residual
        gamma_old = jnp.float32(1.0)
        alpha_old = jnp.float32(1.0)
        for turn in range(ITERS):
            precond = residual / diagonal
            image, unused = apply(precond)
            gamma, delta = lax.psum(
                (jnp.sum(residual * precond), jnp.sum(image * precond)), ("sec", "gx")
            )
            if turn == 0:
                alpha = gamma / delta
                direction = precond
                along = image
            else:
                ratio = gamma / gamma_old
                alpha = gamma / (delta - ratio * gamma / alpha_old)
                direction = precond + ratio * direction
                along = image + ratio * along
            iterate = iterate + alpha * direction
            residual = residual - alpha * along
            gamma_old = gamma
            alpha_old = alpha
        head = iterate
    return (head, jnp.stack(flows)[None])


def solution(mesh):
    placed = (P("sec", "gx", None), P("sec", "gx", None), P(), P(), P(None, "gx", None))
    return jax.shard_map(
        body,
        mesh=mesh,
        in_specs=placed,
        out_specs=(P("sec", "gx", None), P("sec", None, "gx", None)),
        check_vma=False,
    )
```

profile of v0, /device:TPU:0, one launch (start us, length us, event | category | flops | bytes accessed | tf_op | source)
XLA Modules:
  0.0 910.7 jit_solution(3671066435199770177)
XLA Ops:
  2.4 9.2 %add_multiply_fusion.2 = (f32[4,16,1024]{2,1,0:T(8,128)S(1)}, f32[4,16,1024]{2,1,0:T(8,128)S(1)}, pred[4,16,1024]{2,1,0:T(8,128)(4,1)S(1)}, pred[4,16,1024]{2,1,...) fusion(f32[4,16,1024]{2,1,0:T(8,128)} %param.29, ...), kind=kLoop, calls=%fused_computation.667 | loop fusion | flops 2015232 | bytes 1900592 | tf_op jit(solution)/shard_map/mul | solution.py:94
  13.0 5.5 collective-permute-start
  18.6 10.5 %all-gather = f32[64,1024]{1,0:T(8,128)S(1)} all-gather(f32[16,1024]{1,0:T(8,128)S(1)} %get-tuple-element.1115), channel_id=2, replica_groups=mesh['sec'=4,'gx'=8] {'sec'}, dimensions={0}, use_global_device_ids=true | all-gather | bytes 327680 | tf_op jit(solution)/shard_map/all_gather | solution.py:11
  29.3 7.8 all-gather.1
  37.0 9.3 %all_gather.52 = f32[4,16,1024]{2,1,0:T(8,128)S(1)} all-gather(f32[1,16,1024]{2,1,0:T(8,128)S(1)} %slice_multiply_fusion.2), channel_id=1, replica_groups=mesh['sec'=4,'gx'=8] {'sec'}, dimensions={0}, use_global_device_ids=true | all-gather | bytes 327680 | tf_op jit(solution)/shard_map/all_gather | solution.py:11
  48.6 3.0 collective-permute-start.2
  52.8 8.9 fusion.417
  63.0 4.6 collective-permute-start.4
  72.4 3.1 collective-permute-start.6
  78.1 44.2 %all-reduce.44 = (f32[]{:T(128)}, f32[]{:T(128)}) all-reduce(f32[]{:T(128)} %get-tuple-element.874, f32[]{:T(128)} %get-tuple-element.873), channel_id=1, replica_groups=mesh['sec'=4,'gx'=8] {'sec','gx'}, use_global_device_ids=true, to_apply=%region_6.7 | all-reduce | flops 2 | bytes 16 | tf_op jit(solution)/shard_map/psum | solution.py:130
  125.0 4.8 collective-permute-start.8
  133.9 3.0 collective-permute-start.10
  139.5 44.4 %all-reduce.43 = (f32[]{:T(128)}, f32[]{:T(128)}) all-reduce(f32[]{:T(128)} %get-tuple-element.872, f32[]{:T(128)} %get-tuple-element.871), channel_id=1, replica_groups=mesh['sec'=4,'gx'=8] {'sec','gx'}, use_global_device_ids=true, to_apply=%region_10.11 | all-reduce | flops 2 | bytes 16 | tf_op jit(solution)/shard_map/psum | solution.py:130
  190.0 4.8 collective-permute-start.12
  198.7 3.0 collective-permute-start.14
  205.0 43.5 %all-reduce.42 = (f32[]{:T(128)}, f32[]{:T(128)}) all-reduce(f32[]{:T(128)} %get-tuple-element.870, f32[]{:T(128)} %get-tuple-element.869), channel_id=1, replica_groups=mesh['sec'=4,'gx'=8] {'sec','gx'}, use_global_device_ids=true, to_apply=%region_14.15 | all-reduce | flops 2 | bytes 16 | tf_op jit(solution)/shard_map/psum | solution.py:130
  255.5 4.8 collective-permute-start.16
  264.3 3.2 collective-permute-start.18
  270.7 44.4 %all-reduce.41 = (f32[]{:T(128)}, f32[]{:T(128)}) all-reduce(f32[]{:T(128)} %get-tuple-element.868, f32[]{:T(128)} %get-tuple-element.867), channel_id=1, replica_groups=mesh['sec'=4,'gx'=8] {'sec','gx'}, use_global_device_ids=true, to_apply=%region_18.19 | all-reduce | flops 2 | bytes 16 | tf_op jit(solution)/shard_map/psum | solution.py:130
  320.6 4.8 collective-permute-start.20
  325.5 10.7 %all-gather.2 = f32[64,1024]{1,0:T(8,128)S(1)} all-gather(f32[16,1024]{1,0:T(8,128)S(1)} %get-tuple-element.989), channel_id=4, replica_groups=mesh['sec'=4,'gx'=8] {'sec'}, dimensions={0}, use_global_device_ids=true | all-gather | bytes 327680 | tf_op jit(solution)/shard_map/all_gather | solution.py:11
  336.4 7.6 all-gather.3
  343.9 9.5 %all_gather.57 = f32[4,16,1024]{2,1,0:T(8,128)S(1)} all-gather(f32[1,16,1024]{2,1,0:T(8,128)S(1)} %slice_multiply_fusion.1), channel_id=1, replica_groups=mesh['sec'=4,'gx'=8] {'sec'}, dimensions={0}, use_global_device_ids=true | all-gather | bytes 327680 | tf_op jit(solution)/shard_map/all_gather | solution.py:11
  355.3 3.0 collective-permute-start.22
  361.8 4.6 collective-permute-start.24
  370.8 3.0 collective-permute-start.26
  376.5 43.0 %all-reduce.40 = (f32[]{:T(128)}, f32[]{:T(128)}) all-reduce(f32[]{:T(128)} %get-tuple-element.866, f32[]{:T(128)} %get-tuple-element.865), channel_id=1, replica_groups=mesh['sec'=4,'gx'=8] {'sec','gx'}, use_global_device_ids=true, to_apply=%region_27.28 | all-reduce | flops 2 | bytes 16 | tf_op jit(solution)/shard_map/psum | solution.py:130
  422.2 4.8 collective-permute-start.28
  431.1 3.0 collective-permute-start.30
  436.7 44.4 %all-reduce.39 = (f32[]{:T(128)}, f32[]{:T(128)}) all-reduce(f32[]{:T(128)} %get-tuple-element.864, f32[]{:T(128)} %get-tuple-element.863), channel_id=1, replica_groups=mesh['sec'=4,'gx'=8] {'sec','gx'}, use_global_device_ids=true, to_apply=%region_31.32 | all-reduce | flops 2 | bytes 16 | tf_op jit(solution)/shard_map/psum | solution.py:130
  487.1 4.8 collective-permute-start.32
  495.9 3.0 collective-permute-start.34
  502.2 43.5 %all-reduce.38 = (f32[]{:T(128)}, f32[]{:T(128)}) all-reduce(f32[]{:T(128)} %get-tuple-element.862, f32[]{:T(128)} %get-tuple-element.861), channel_id=1, replica_groups=mesh['sec'=4,'gx'=8] {'sec','gx'}, use_global_device_ids=true, to_apply=%region_35.36 | all-reduce | flops 2 | bytes 16 | tf_op jit(solution)/shard_map/psum | solution.py:130
  552.6 4.8 collective-permute-start.36
  561.5 3.2 collective-permute-start.38
  568.0 44.3 %all-reduce.37 = (f32[]{:T(128)}, f32[]{:T(128)}) all-reduce(f32[]{:T(128)} %get-tuple-element.860, f32[]{:T(128)} %get-tuple-element.859), channel_id=1, replica_groups=mesh['sec'=4,'gx'=8] {'sec','gx'}, use_global_device_ids=true, to_apply=%region_39.40 | all-reduce | flops 2 | bytes 16 | tf_op jit(solution)/shard_map/psum | solution.py:130
  617.7 4.8 collective-permute-start.40
  622.5 10.7 %all-gather.4 = f32[64,1024]{1,0:T(8,128)S(1)} all-gather(f32[16,1024]{1,0:T(8,128)S(1)} %get-tuple-element.972), channel_id=6, replica_groups=mesh['sec'=4,'gx'=8] {'sec'}, dimensions={0}, use_global_device_ids=true | all-gather | bytes 327680 | tf_op jit(solution)/shard_map/all_gather | solution.py:11
  633.5 7.6 all-gather.5
  641.1 9.5 %all_gather.62 = f32[4,16,1024]{2,1,0:T(8,128)S(1)} all-gather(f32[1,16,1024]{2,1,0:T(8,128)S(1)} %slice_multiply_fusion), channel_id=1, replica_groups=mesh['sec'=4,'gx'=8] {'sec'}, dimensions={0}, use_global_device_ids=true | all-gather | bytes 327680 | tf_op jit(solution)/shard_map/all_gather | solution.py:11
  658.9 4.6 collective-permute-start.44
  673.6 43.0 %all-reduce.36 = (f32[]{:T(128)}, f32[]{:T(128)}) all-reduce(f32[]{:T(128)} %get-tuple-element.858, f32[]{:T(128)} %get-tuple-element.857), channel_id=1, replica_groups=mesh['sec'=4,'gx'=8] {'sec','gx'}, use_global_device_ids=true, to_apply=%region_48.49 | all-reduce | flops 2 | bytes 16 | tf_op jit(solution)/shard_map/psum | solution.py:130
  719.2 4.8 collective-permute-start.48
  733.7 44.4 %all-reduce.35 = (f32[]{:T(128)}, f32[]{:T(128)}) all-reduce(f32[]{:T(128)} %get-tuple-element.856, f32[]{:T(128)} %get-tuple-element.855), channel_id=1, replica_groups=mesh['sec'=4,'gx'=8] {'sec','gx'}, use_global_device_ids=true, to_apply=%region_52.53 | all-reduce | flops 2 | bytes 16 | tf_op jit(solution)/shard_map/psum | solution.py:130
  783.9 4.8 collective-permute-start.52
  798.3 43.5 %all-reduce.34 = (f32[]{:T(128)}, f32[]{:T(128)}) all-reduce(f32[]{:T(128)} %get-tuple-element.854, f32[]{:T(128)} %get-tuple-element.853), channel_id=1, replica_groups=mesh['sec'=4,'gx'=8] {'sec','gx'}, use_global_device_ids=true, to_apply=%region_56.57 | all-reduce | flops 2 | bytes 16 | tf_op jit(solution)/shard_map/psum | solution.py:130
  847.0 4.8 collective-permute-start.56
  861.4 44.3 %all-reduce.33 = (f32[]{:T(128)}, f32[]{:T(128)}) all-reduce(f32[]{:T(128)} %get-tuple-element.852, f32[]{:T(128)} %get-tuple-element.851), channel_id=1, replica_groups=mesh['sec'=4,'gx'=8] {'sec','gx'}, use_global_device_ids=true, to_apply=%region_60.61 | all-reduce | flops 2 | bytes 16 | tf_op jit(solution)/shard_map/psum | solution.py:130
  (277 shorter events, 136.9 us)
Async XLA Ops:
  11.7 35.0 %collective-permute-start.1 = (f32[2,1,16,1024]{3,2,1,0:T(8,128)S(1)}, f32[2,1,16,1024]{3,2,1,0:T(8,128)S(1)}, u32[]{:S(2)}, u32[]{:S(2)}) collective-permute-start(f32[2,1,16,1024]{3,2,1,0:T(8,128)S(1)} %get-tuple-element.1007), channel_id=1, source_target_pairs={{8,0},{16,8},{24,16},{9,1},{17,9},{25,17},{10,2},{18,10},{26,18},{... | collective-permute-start | bytes 393224 | tf_op jit(solution)/shard_map/ppermute | solution.py:35
  13.0 33.7 %collective-permute-start = (f32[2,1,16,1024]{3,2,1,0:T(8,128)S(1)}, f32[2,1,16,1024]{3,2,1,0:T(8,128)S(1)}, u32[]{:S(2)}, u32[]{:S(2)}) collective-permute-start(f32[2,1,16,1024]{3,2,1,0:T(8,128)S(1)} %get-tuple-element.1116), channel_id=1, source_target_pairs={{0,8},{8,16},{16,24},{1,9},{9,17},{17,25},{2,10},{10,18},{18,26},{... | collective-permute-start | bytes 393224 | tf_op jit(solution)/shard_map/ppermute | solution.py:32
  47.3 5.0 collective-permute-start.3
  48.6 3.9 collective-permute-start.2
  61.7 7.5 collective-permute-start.5
  63.0 7.9 collective-permute-start.4
  71.1 4.5 collective-permute-start.7
  72.4 4.0 collective-permute-start.6
  123.7 7.6 collective-permute-start.9
  125.0 7.4 collective-permute-start.8
  132.6 4.3 collective-permute-start.11
  133.9 3.9 collective-permute-start.10
  188.7 7.4 collective-permute-start.13
  190.0 7.3 collective-permute-start.12
  197.4 4.3 collective-permute-start.15
  254.2 7.5 collective-permute-start.17
  255.5 7.4 collective-permute-start.16
  263.0 4.5 collective-permute-start.19
  319.3 34.5 %collective-permute-start.21 = (f32[2,1,16,1024]{3,2,1,0:T(8,128)S(1)}, f32[2,1,16,1024]{3,2,1,0:T(8,128)S(1)}, u32[]{:S(2)}, u32[]{:S(2)}) collective-permute-start(f32[2,1,16,1024]{3,2,1,0:T(8,128)S(1)} %get-tuple-element.991), channel_id=1, source_target_pairs={{8,0},{16,8},{24,16},{9,1},{17,9},{25,17},{10,2},{18,10},{26,18},{... | collective-permute-start | bytes 393224 | tf_op jit(solution)/shard_map/ppermute | solution.py:35
  320.6 33.2 %collective-permute-start.20 = (f32[2,1,16,1024]{3,2,1,0:T(8,128)S(1)}, f32[2,1,16,1024]{3,2,1,0:T(8,128)S(1)}, u32[]{:S(2)}, u32[]{:S(2)}) collective-permute-start(f32[2,1,16,1024]{3,2,1,0:T(8,128)S(1)} %get-tuple-element.1106), channel_id=1, source_target_pairs={{0,8},{8,16},{16,24},{1,9},{9,17},{17,25},{2,10},{10,18},{18,26},{... | collective-permute-start | bytes 393224 | tf_op jit(solution)/shard_map/ppermute | solution.py:32
  354.0 4.4 collective-permute-start.23
  360.5 8.0 collective-permute-start.25
  361.8 7.6 collective-permute-start.24
  369.5 4.3 collective-permute-start.27
  420.9 7.6 collective-permute-start.29
  422.2 7.4 collective-permute-start.28
  429.8 4.3 collective-permute-start.31
  485.8 7.5 collective-permute-start.33
  487.1 7.3 collective-permute-start.32
  494.6 4.3 collective-permute-start.35
  551.3 7.5 collective-permute-start.37
  552.6 7.4 collective-permute-start.36
  560.2 4.6 collective-permute-start.39
  616.4 34.5 %collective-permute-start.41 = (f32[2,1,16,1024]{3,2,1,0:T(8,128)S(1)}, f32[2,1,16,1024]{3,2,1,0:T(8,128)S(1)}, u32[]{:S(2)}, u32[]{:S(2)}) collective-permute-start(f32[2,1,16,1024]{3,2,1,0:T(8,128)S(1)} %get-tuple-element.974), channel_id=1, source_target_pairs={{8,0},{16,8},{24,16},{9,1},{17,9},{25,17},{10,2},{18,10},{26,18},{... | collective-permute-start | bytes 393224 | tf_op jit(solution)/shard_map/ppermute | solution.py:35
  617.7 33.2 %collective-permute-start.40 = (f32[2,1,16,1024]{3,2,1,0:T(8,128)S(1)}, f32[2,1,16,1024]{3,2,1,0:T(8,128)S(1)}, u32[]{:S(2)}, u32[]{:S(2)}) collective-permute-start(f32[2,1,16,1024]{3,2,1,0:T(8,128)S(1)} %get-tuple-element.1097), channel_id=1, source_target_pairs={{0,8},{8,16},{16,24},{1,9},{9,17},{17,25},{2,10},{10,18},{18,26},{... | collective-permute-start | bytes 393224 | tf_op jit(solution)/shard_map/ppermute | solution.py:32
  651.1 4.4 collective-permute-start.43
  657.6 8.0 collective-permute-start.45
  658.9 7.7 collective-permute-start.44
  666.6 4.3 collective-permute-start.47
  717.9 7.5 collective-permute-start.49
  719.2 7.4 collective-permute-start.48
  726.8 4.3 collective-permute-start.51
  782.6 7.5 collective-permute-start.53
  783.9 7.4 collective-permute-start.52
  791.4 4.3 collective-permute-start.55
  845.7 7.5 collective-permute-start.57
  847.0 7.3 collective-permute-start.56
  854.5 5.1 collective-permute-start.59
  (23 other events, 125.4 us)
where the time goes:
time: 923 us; the launch traced here: 911 us
  blocking collectives  610 us (66%)
  starting transfers between devices  157 us (17%)
  other arithmetic  49.4 us (5%)
  waiting for transfers between devices  43.5 us (5%)
  between operations  43.4 us (5%)
    psum x12, blocking collectives, body(): lax.psum((jnp.sum(residual * precond), jnp.sum(image * precond)), ('sec',...  527 us
    ppermute x30, starting transfers between devices, padded_2(): lax.ppermute(lax.slice_in_dim(block, block.shape[dim] - width, None, axis...  118 us
    all_gather x9, blocking collectives, prefix(): everything = jax.tree.map(lambda part: lax.all_gather(part, axis), shard)  83.2 us
    ppermute x30, starting transfers between devices, padded_2(): lax.ppermute(lax.slice_in_dim(block, 0, width, axis=dim), axis, backward)  38.8 us
    ppermute x30, waiting for transfers between devices, padded_2(): lax.ppermute(lax.slice_in_dim(block, block.shape[dim] - width, None, axis...  25.1 us
  transfers between devices with their start and end apart: 60, of which 39 were waited for; matrix products, arithmetic and copies ran while one was open for 0% of the time, Pallas kernels for 0%

commit v1 on v0

v1 whole, which is shorter than its diff:
```python
import functools

import jax
import jax.numpy as jnp
from jax import lax
from jax.experimental import pallas as pl
from jax.experimental.pallas import tpu as pltpu
from jax.sharding import PartitionSpec as P


MESH = pl.DeviceIdType.MESH
RIM = 8
LANES = 128
ITERS = 4


def place_of(s):
    return s + s // 2 - 2 * (s // 3)


def coefficients(g, h):
    nu = [g[0], h[0]]
    for k in range(1, ITERS):
        nu.append(2.0 * g[k] - nu[0])
        nu.append(4.0 * h[k] - 2.0 * nu[1] - nu[2 * k - 1])

    def gram(i, j):
        return 0.5 * (nu[i + j] + nu[abs(i - j)])

    def gram_a(i, j):
        shifted = gram(i, 1) if j == 0 else 0.5 * (gram(i, j + 1) + gram(i, j - 1))
        return gram(i, j) - shifted

    G = [[gram(i, j) for j in range(ITERS)] for i in range(ITERS)]
    H = [[gram_a(max(i, j), min(i, j)) for j in range(ITERS)] for i in range(ITERS)]
    zero = jnp.zeros_like(g[0])

    def form(matrix, v, top):
        total = zero
        for i in range(top + 1):
            row = matrix[i][i] * v[i]
            for j in range(i):
                row = row + 2.0 * matrix[i][j] * v[j]
            total = total + row * v[i]
        return total

    z = [zero + 1.0] + [zero] * (ITERS - 1)
    p = list(z)
    x = [zero] * ITERS
    rz = nu[0]
    for k in range(ITERS):
        curve = form(H, p, k)
        alpha = jnp.where(curve > 0.0, rz / jnp.where(curve > 0.0, curve, 1.0), 0.0)
        x = [a + alpha * b for a, b in zip(x, p)]
        if k + 1 < ITERS:
            image = list(p)
            for i in range(k + 1):
                if i == 0:
                    image[1] = image[1] - p[0]
                else:
                    image[i + 1] = image[i + 1] - 0.5 * p[i]
                    image[i - 1] = image[i - 1] - 0.5 * p[i]
            z = [a - alpha * b for a, b in zip(z, image)]
            new = jnp.maximum(form(G, z, k + 1), 0.0)
            beta = jnp.where(rz > 0.0, new / jnp.where(rz > 0.0, rz, 1.0), 0.0)
            p = [a + beta * b for a, b in zip(z, p)]
            rz = new
    return x


def kernel(
    n_sec, n_gx, steps, kinds,
    start_ref, soil_ref, cond_ref, store_ref, rain_ref,
    out_ref, flow_ref,
    kind_mine, head, kind, store, cond, cap, face_l, face_r, face_c, diag, dinv, t0, t1, t2, t3,
    water, enter, leave, rainx, flows, pack_out, pack_in, stat_a, stat_b,
    own_sem, swap_send, swap_recv, col_send, col_recv, row_send, row_recv,
    a_send, a_recv, b_send, b_recv, back_send, back_recv,
):
    f32 = jnp.float32
    layers, rows, wide = start_ref.shape
    cols = wide // n_sec
    total = layers * n_sec
    sec, gx = lax.axis_index("sec"), lax.axis_index("gx")
    here = place_of(sec)
    ext_r, ext_c = rows + 2 * RIM, cols + LANES
    own = (slice(0, rows), slice(0, cols))

    def at(place):
        return pl.ds(pl.multiple_of(place * cols, LANES), cols)

    def layers_of(s):
        return pl.ds(1 + s * layers, layers)

    plane = jnp.zeros((ext_r, ext_c), f32)
    for ref in (head, kind, cond, t0, t1, t2, t3, face_l):
        ref[0] = plane
        ref[total + 1] = plane

    def clear(l, carry):
        for ref in (head, kind):
            ref[l, rows:, :] = jnp.zeros((2 * RIM, ext_c), f32)
        return carry

    lax.fori_loop(1, total + 1, clear, 0)
    for c in range(steps):
        rainx[c] = plane
    pack_in[...] = jnp.zeros_like(pack_in)
    kind_mine[...] = soil_ref[...].astype(f32) + 1.0

    sec_peers = [lax.rem(sec + k, n_sec) for k in range(1, n_sec)]
    gx_peers = [lax.rem(gx + k, n_gx) for k in range(1, n_gx)]
    barrier = pltpu.get_barrier_semaphore()
    for peer in sec_peers:
        pl.semaphore_signal(barrier, inc=1, device_id={"sec": peer}, device_id_type=MESH)
    for peer in gx_peers:
        pl.semaphore_signal(barrier, inc=1, device_id={"gx": peer}, device_id_type=MESH)

    lane = lax.broadcasted_iota(jnp.int32, (rows, LANES), 1)
    after = pl.multiple_of(lax.rem(here + 1, n_sec) * cols, LANES)
    before = pl.multiple_of(lax.rem(here + n_sec - 1, n_sec) * cols + cols - LANES, LANES)
    for c in range(steps):
        rainx[c, 0:rows, 0:cols] = rain_ref[c, :, at(here)]
        rainx[c, 0:rows, cols:] = jnp.where(
            lane < LANES // 2, rain_ref[c, :, pl.ds(after, LANES)], rain_ref[c, :, pl.ds(before, LANES)]
        )
    pl.semaphore_wait(barrier, n_sec + n_gx - 2)

    moves = []
    for f, (src, dst) in enumerate(((start_ref, head), (kind_mine, kind))):
        copy = pltpu.make_async_copy(
            src.at[:, :, at(here)], dst.at[layers_of(sec), 0:rows, 0:cols], own_sem.at[f]
        )
        copy.start()
        moves.append(copy)
        for k, peer in enumerate(sec_peers):
            copy = pltpu.make_async_remote_copy(
                src_ref=src.at[:, :, at(place_of(peer))],
                dst_ref=dst.at[layers_of(sec), 0:rows, 0:cols],
                send_sem=swap_send.at[f, k],
                recv_sem=swap_recv.at[f, k],
                device_id={"sec": peer},
                device_id_type=MESH,
            )
            copy.start()
            moves.append(copy)
    for copy in moves:
        copy.wait()

    def packed(field, low):
        outs = jnp.zeros((rows, LANES), f32)
        for l in range(total):
            if low:
                tile = field[1 + l, 0:rows, 0:LANES]
                shift = RIM * l
            else:
                tile = field[1 + l, 0:rows, cols - LANES:cols]
                shift = (RIM * l + RIM) % LANES
            moved = pltpu.roll(tile, shift, 1) if shift else tile
            outs = jnp.where(lane // RIM == l, moved, outs)
        return outs

    def send_cols(slot, field):
        pack_out[slot, 0] = packed(field, True)
        pack_out[slot, 1] = packed(field, False)
        for d in (0, 1):
            @pl.when(here > 0 if d == 0 else here < n_sec - 1)
            def _(d=d):
                col_copy(slot, d).start()

    def col_copy(slot, d):
        return pltpu.make_async_remote_copy(
            src_ref=pack_out.at[slot, d],
            dst_ref=pack_in.at[slot, d],
            send_sem=col_send.at[slot, d],
            recv_sem=col_recv.at[slot, d],
            device_id={"sec": place_of(lax.rem(here + n_sec - 1, n_sec) if d == 0 else lax.rem(here + 1, n_sec))},
            device_id_type=MESH,
        )

    def take_cols(slot, field):
        @pl.when(here > 0)
        def _():
            col_copy(slot, 0).wait_send()
            col_copy(slot, 1).wait_recv()

        @pl.when(here < n_sec - 1)
        def _():
            col_copy(slot, 1).wait_send()
            col_copy(slot, 0).wait_recv()

        right, left = pack_in[slot, 0], pack_in[slot, 1]
        for l in range(total):
            a, b = (-RIM * l) % LANES, (LANES - RIM - RIM * l) % LANES
            ra = pltpu.roll(right, a, 1) if a else right
            rb = pltpu.roll(left, b, 1) if b else left
            field[1 + l, 0:rows, cols:] = jnp.where(lane < RIM, ra, jnp.where(lane >= LANES - RIM, rb, 0.0))

    def row_copy(slot, field, first, count, d):
        src = pl.ds(0, RIM) if d == 0 else pl.ds(rows - RIM, RIM)
        dst = pl.ds(rows, RIM) if d == 0 else pl.ds(rows + RIM, RIM)
        return pltpu.make_async_remote_copy(
            src_ref=field.at[pl.ds(first, count), src, :],
            dst_ref=field.at[pl.ds(first, count), dst, :],
            send_sem=row_send.at[slot, d],
            recv_sem=row_recv.at[slot, d],
            device_id={"gx": lax.rem(gx + n_gx - 1, n_gx) if d == 0 else lax.rem(gx + 1, n_gx)},
            device_id_type=MESH,
        )

    def send_rows(*what):
        for d in (0, 1):
            @pl.when(gx > 0 if d == 0 else gx < n_gx - 1)
            def _(d=d):
                row_copy(*what, d).start()

    def take_rows(*what):
        @pl.when(gx > 0)
        def _():
            row_copy(*what, 0).wait_send()
            row_copy(*what, 1).wait_recv()

        @pl.when(gx < n_gx - 1)
        def _():
            row_copy(*what, 1).wait_send()
            row_copy(*what, 0).wait_recv()

    def shift(v, by, axis):
        return pltpu.roll(v, by % v.shape[axis], axis)

    def harmonic(a, b):
        return 2.0 * a * b / jnp.maximum(a + b, 1e-30)

    def folded(v):
        out = None
        for i in range(0, rows, RIM):
            for j in range(0, cols, LANES):
                part = v[i:i + RIM, j:j + LANES]
                out = part if out is None else out + part
        return out

    none = jnp.zeros((RIM, LANES), f32)
    basis = (t0, t1, t2, t3)

    for c in range(steps):
        send_cols(c, head)
        if c == 0:
            send_cols(steps, kind)
            send_rows(steps + 1, rainx, 0, steps)
        take_cols(c, head)
        send_rows(c, head, 1, total)
        if c == 0:
            take_cols(steps, kind)
            send_rows(steps, kind, 1, total)
            take_rows(steps + 1, rainx, 0, steps)
            take_rows(steps, kind, 1, total)

            def look(l, carry):
                here_kind = kind[l]
                a = jnp.zeros((ext_r, ext_c), f32)
                b = jnp.zeros((ext_r, ext_c), f32)
                for k in range(kinds):
                    same = here_kind == jnp.float32(k + 1)
                    a = jnp.where(same, cond_ref[k], a)
                    b = jnp.where(same, store_ref[k], b)
                kind[l] = a
                store[l] = b
                return carry

            lax.fori_loop(1, total + 1, look, 0)
        take_rows(c, head, 1, total)

        def soil(s, carry):
            amount = jnp.zeros((ext_r, ext_c), f32)
            for j in range(layers):
                l = 1 + s * layers + j
                sat = jax.nn.sigmoid(head[l])
                cond[l] = kind[l] * (0.05 + sat * sat)
                cap[l] = store[l] * (0.1 + sat * (1.0 - sat))
                amount = amount + sat
            water[s] = amount
            return carry

        lax.fori_loop(0, n_sec, soil, 0)

        depth = jnp.float32(layers)
        below = jnp.zeros((ext_r, ext_c), f32)
        for s in reversed(range(n_sec)):
            amount = water[s]
            water[s] = amount / depth * (0.5 + 0.5 * below / (below + depth))
            below = below + amount
        entering = rainx[c]
        for s in range(n_sec):
            enter[s] = entering
            flows[s, c] = entering[own]
            entering = water[s] * entering + 0.5 * cond[(s + 1) * layers]
            leave[s] = entering

        def faces(l, carry):
            k = cond[l]
            face_l[l] = harmonic(k, cond[l + 1])
            face_r[l] = harmonic(k, shift(k, -1, 0))
            face_c[l] = harmonic(k, shift(k, -1, 1))
            return carry

        lax.fori_loop(1, total + 1, faces, 0)

        def first(s, acc):
            for j in range(layers):
                l = 1 + s * layers + j
                up, down = face_l[l - 1], face_l[l]
                fr, fc = face_r[l], face_c[l]
                v = head[l]
                whole = cap[l] + up + down + fr + shift(fr, 1, 0) + fc + shift(fc, 1, 1)
                flux_r = fr * (shift(v, -1, 0) - v)
                flux_c = fc * (shift(v, -1, 1) - v)
                res = up - down + up * (head[l - 1] - v) + down * (head[l + 1] - v)
                res = res + flux_r - shift(flux_r, 1, 0) + flux_c - shift(flux_c, 1, 1)
                if j == 0:
                    res = res + enter[s]
                if j == layers - 1:
                    res = res - leave[s]
                inverse = jnp.where(whole > 0.0, 1.0 / jnp.maximum(whole, 1e-30), 0.0)
                z = res * inverse
                diag[l] = whole
                dinv[l] = inverse
                t0[l] = z
                acc = acc + folded(res * z)
            return acc

        g = [lax.fori_loop(0, n_sec, first, none)]
        h = []
        for k in range(ITERS):
            def apply(l, acc, k=k):
                t = basis[k]
                fr, fc = face_r[l], face_c[l]
                v = t[l]
                near = face_l[l - 1] * t[l - 1] + face_l[l] * t[l + 1]
                near = near + fr * shift(v, -1, 0) + shift(fr * v, 1, 0)
                near = near + fc * shift(v, -1, 1) + shift(fc * v, 1, 1)
                ah = acc[0] + folded(v * near)
                ag = acc[1]
                if k + 1 < ITERS:
                    new = dinv[l] * near
                    if k > 0:
                        new = 2.0 * new - basis[k - 1][l]
                    basis[k + 1][l] = new
                    ag = ag + folded(diag[l] * new * new)
                return (ah, ag)

            ah, ag = lax.fori_loop(1, total + 1, apply, (none, none))
            h.append(ah)
            if k + 1 < ITERS:
                g.append(ag)

        flat = [jnp.sum(v, axis=0, keepdims=True) for v in g + h]
        stat_a[c, sec] = jnp.concatenate(flat, axis=0)
        sends = []
        for k, peer in enumerate(sec_peers):
            copy = pltpu.make_async_remote_copy(
                src_ref=stat_a.at[c, sec],
                dst_ref=stat_a.at[c, sec],
                send_sem=a_send.at[c, k],
                recv_sem=a_recv.at[c, k],
                device_id={"sec": peer},
                device_id_type=MESH,
            )
            copy.start()
            sends.append(copy)
        for copy in sends:
            copy.wait()
        summed = stat_a[c, 0]
        for k in range(1, n_sec):
            summed = summed + stat_a[c, k]
        stat_b[c, gx] = summed
        sends = []
        for k, peer in enumerate(gx_peers):
            copy = pltpu.make_async_remote_copy(
                src_ref=stat_b.at[c, gx],
                dst_ref=stat_b.at[c, gx],
                send_sem=b_send.at[c, k],
                recv_sem=b_recv.at[c, k],
                device_id={"gx": peer},
                device_id_type=MESH,
            )
            copy.start()
            sends.append(copy)
        for copy in sends:
            copy.wait()
        summed = stat_b[c, 0]
        for k in range(1, n_gx):
            summed = summed + stat_b[c, k]
        sums = jnp.sum(summed, axis=1, keepdims=True)
        parts = [sums[k:k + 1] for k in range(2 * ITERS)]
        x = coefficients(parts[:ITERS], parts[ITERS:])
        x = [jnp.broadcast_to(v, (rows, cols)) for v in x]

        def update(l, carry):
            v = head[l, 0:rows, 0:cols]
            for k in range(ITERS):
                v = v + x[k] * basis[k][l, 0:rows, 0:cols]
            head[l, 0:rows, 0:cols] = v
            return carry

        lax.fori_loop(1, total + 1, update, 0)

    moves = []
    for f in range(2):
        def src(s):
            return head.at[layers_of(s), 0:rows, 0:cols] if f == 0 else flows.at[s]

        dst = out_ref.at[:, :, at(here)] if f == 0 else flow_ref.at[0, :, :, at(here)]
        copy = pltpu.make_async_copy(src(sec), dst, own_sem.at[2 + f])
        copy.start()
        moves.append(copy)
        for k, peer in enumerate(sec_peers):
            copy = pltpu.make_async_remote_copy(
                src_ref=src(peer),
                dst_ref=dst,
                send_sem=back_send.at[f, k],
                recv_sem=back_recv.at[f, k],
                device_id={"sec": peer},
                device_id_type=MESH,
            )
            copy.start()
            moves.append(copy)
    for copy in moves:
        copy.wait()


def body(n_sec, n_gx, start, soil, conductivity, storage, rain):
    layers, rows, wide = start.shape
    steps = rain.shape[0]
    cols = wide // n_sec
    total = layers * n_sec
    assert total * RIM <= LANES and cols % LANES == 0 and rows % RIM == 0 and n_sec == 4
    ext = (rows + 2 * RIM, cols + LANES)
    f32 = jnp.float32
    field = pltpu.VMEM((total + 2,) + ext, f32)
    per_sec = pltpu.VMEM((n_sec,) + ext, f32)
    dma = pltpu.SemaphoreType.DMA
    vmem = pl.BlockSpec(memory_space=pltpu.VMEM)
    smem = pl.BlockSpec(memory_space=pltpu.SMEM)
    return tuple(pl.pallas_call(
        functools.partial(kernel, n_sec, n_gx, steps, conductivity.shape[0]),
        out_shape=(
            jax.ShapeDtypeStruct(start.shape, f32),
            jax.ShapeDtypeStruct((1, steps, rows, wide), f32),
        ),
        in_specs=[vmem, vmem, smem, smem, vmem],
        out_specs=(vmem, vmem),
        scratch_shapes=[pltpu.VMEM(start.shape, f32)]
        + [field] * 14
        + [per_sec] * 3
        + [
            pltpu.VMEM((steps,) + ext, f32),
            pltpu.VMEM((n_sec, steps, rows, cols), f32),
            pltpu.VMEM((steps + 1, 2, rows, LANES), f32),
            pltpu.VMEM((steps + 1, 2, rows, LANES), f32),
            pltpu.VMEM((steps, n_sec, 2 * ITERS, LANES), f32),
            pltpu.VMEM((steps, n_gx, 2 * ITERS, LANES), f32),
            dma((4,)),
            dma((2, n_sec - 1)),
            dma((2, n_sec - 1)),
            dma((steps + 1, 2)),
            dma((steps + 1, 2)),
            dma((steps + 2, 2)),
            dma((steps + 2, 2)),
            dma((steps, n_sec - 1)),
            dma((steps, n_sec - 1)),
            dma((steps, n_gx - 1)),
            dma((steps, n_gx - 1)),
            dma((2, n_sec - 1)),
            dma((2, n_sec - 1)),
        ],
        compiler_params=pltpu.CompilerParams(collective_id=0, has_side_effects=True),
    )(start, soil, conductivity, storage, rain))


def solution(mesh):
    placed = (P("sec", "gx", None), P("sec", "gx", None), P(), P(), P(None, "gx", None))
    return jax.shard_map(
        functools.partial(body, mesh.shape["sec"], mesh.shape["gx"]),
        mesh=mesh,
        in_specs=placed,
        out_specs=(P("sec", "gx", None), P("sec", None, "gx", None)),
        check_vma=False,
    )
```

time: 923 us -> 96.3 us (0.10); the launches traced: 911 us -> 96.1 us
  blocking collectives: 610 us -> 0 us
  starting transfers between devices: 157 us -> 0 us
  Pallas kernels: 0 us -> 93.1 us
  other arithmetic: 49.4 us -> 0 us
  waiting for transfers between devices: 43.5 us -> 0 us
  between operations: 43.4 us -> 0.65 us
    psum x12 -> x0, blocking collectives: 527 us -> none  [body(): lax.psum((jnp.sum(residual * precond), jnp.sum(image * precond)), ('sec',...]
    ppermute x60 -> x0, starting transfers between devices: 157 us -> none  [the longest x30 118 us: padded_2(): lax.ppermute(lax.slice_in_dim(block, block.shape[dim] - width, None, axis...]
    pallas_call x0 -> x1, Pallas kernels: none -> 93.1 us  [body(): pl.pallas_call(functools.partial(kernel, n_sec, n_gx, steps, conductivity...]
    all_gather x9 -> x0, blocking collectives: 83.2 us -> none  [prefix(): everything = jax.tree.map(lambda part: lax.all_gather(part, axis), shard)]
    ppermute x60 -> x0, waiting for transfers between devices: 43.5 us -> none  [the longest x30 25.1 us: padded_2(): lax.ppermute(lax.slice_in_dim(block, block.shape[dim] - width, None, axis...]
    reduce_sum x14 -> x0, other arithmetic: 18.5 us -> none  [the longest x12 18.2 us: body(): jnp.sum(image * precond)]
    div x12 -> x0, other arithmetic: 14.8 us -> none  [body(): precond = residual / diagonal]
    mul x9 -> x0, other arithmetic: 9.5 us -> none  [the longest x3 9.41 us: body(): conductivity = cond_table * (0.05 + saturation * saturation)]
  transfers between devices with their start and end apart: 60 -> 0, of which waited for: 39 -> 0; matrix products, arithmetic and copies ran while one was open for 0% -> 0% of each run, Pallas kernels for 0% -> 0%
where the time goes in v1:
time: 96.3 us; the launch traced here: 96.1 us
  Pallas kernels  93.1 us (97%)
  local copies, waits for them, and re-layouts  2.39 us (2%)
    pallas_call x1, Pallas kernels, body(): pl.pallas_call(functools.partial(kernel, n_sec, n_gx, steps, conductivity...  93.1 us
    unnamed x4, local copies, waits for them, and re-layouts  2.39 us

profile of v1, /device:TPU:0, one launch (start us, length us, event | category | flops | bytes accessed | tf_op | source)
XLA Modules:
  0.0 96.1 jit_solution(18305484202783887695)
XLA Ops:
  0.6 93.1 %shard_map.68 = (f32[4,16,1024]{2,1,0:T(8,128)}, f32[1,3,16,1024]{3,2,1,0:T(8,128)}) custom-call(f32[4,16,1024]{2,1,0:T(8,128)} %start_ref.1, s32[4,16,1024]{2,1,0:T(8,128)} %soil_ref.1, f32[12]{0:T(128)} %cond_ref.1, f32[12]{0:T(128)} %store_ref.1, f32[3,16,1024]{2,1,0:T(8,128)} %rain_ref.1), custom_call_target="tpu_custom_call" | custom-call | tf_op jit(solution)/shard_map/pallas_call | solution.py:444
  93.7 0.0 copy-start
  93.7 1.7 %copy.9 = f32[4,16,1024]{2,1,0:T(8,128)} copy(f32[4,16,1024]{2,1,0:T(8,128)} %get-tuple-element.4) | data formatting | bytes 524288
  95.4 0.0 copy-done
  95.4 0.7 copy.10
Async XLA Ops:
  93.7 1.7 %copy-start = (f32[1,3,16,1024]{3,2,1,0:T(8,128)S(1)}, f32[1,3,16,1024]{3,2,1,0:T(8,128)}, u32[]{:S(2)}) copy-start(f32[1,3,16,1024]{3,2,1,0:T(8,128)} %get-tuple-element.5) | copy-start | bytes 589828

commit v2 on v1

--- a/solution.py
+++ b/solution.py
@@ -73,9 +73,9 @@
     start_ref, soil_ref, cond_ref, store_ref, rain_ref,
     out_ref, flow_ref,
     kind_mine, head, kind, store, cond, cap, face_l, face_r, face_c, diag, dinv, t0, t1, t2, t3,
-    water, enter, leave, rainx, flows, pack_out, pack_in, stat_a, stat_b,
-    own_sem, swap_send, swap_recv, col_send, col_recv, row_send, row_recv,
-    a_send, a_recv, b_send, b_recv, back_send, back_recv,
+    water, enter, leave, rainx, flows, pack_out, pack_in, landed, stats,
+    own_sem, swap_send, swap_recv, col_send, col_recv, row_send, row_recv, land_send, land_recv,
+    sum_send, sum_recv, flow_send, flow_recv, back_send, back_recv,
 ):
     f32 = jnp.float32
     layers, rows, wide = start_ref.shape
@@ -108,26 +108,40 @@
     pack_in[...] = jnp.zeros_like(pack_in)
     kind_mine[...] = soil_ref[...].astype(f32) + 1.0
 
+    @pl.when(jnp.logical_or(gx == 0, gx == n_gx - 1))
+    def _():
+        def wipe(l, carry):
+            for c in range(steps - 1):
+                for k in range(ITERS):
+                    for d in (0, 1):
+                        landed[c, k, d, l] = jnp.zeros((RIM, cols), f32)
+            return carry
+
+        lax.fori_loop(0, total, wipe, 0)
+
     sec_peers = [lax.rem(sec + k, n_sec) for k in range(1, n_sec)]
-    gx_peers = [lax.rem(gx + k, n_gx) for k in range(1, n_gx)]
+    everyone = [
+        {"sec": lax.rem(sec + i, n_sec), "gx": lax.rem(gx + j, n_gx)}
+        for j in range(n_gx) for i in range(n_sec) if i + j
+    ]
     barrier = pltpu.get_barrier_semaphore()
-    for peer in sec_peers:
-        pl.semaphore_signal(barrier, inc=1, device_id={"sec": peer}, device_id_type=MESH)
-    for peer in gx_peers:
-        pl.semaphore_signal(barrier, inc=1, device_id={"gx": peer}, device_id_type=MESH)
-
-    lane = lax.broadcasted_iota(jnp.int32, (rows, LANES), 1)
+    for peer in everyone:
+        pl.semaphore_signal(barrier, inc=1, device_id=peer, device_id_type=MESH)
+
+    lane = lax.broadcasted_iota(jnp.int32, (ext_r, LANES), 1)
     after = pl.multiple_of(lax.rem(here + 1, n_sec) * cols, LANES)
     before = pl.multiple_of(lax.rem(here + n_sec - 1, n_sec) * cols + cols - LANES, LANES)
     for c in range(steps):
         rainx[c, 0:rows, 0:cols] = rain_ref[c, :, at(here)]
         rainx[c, 0:rows, cols:] = jnp.where(
-            lane < LANES // 2, rain_ref[c, :, pl.ds(after, LANES)], rain_ref[c, :, pl.ds(before, LANES)]
+            lane[0:rows] < LANES // 2, rain_ref[c, :, pl.ds(after, LANES)], rain_ref[c, :, pl.ds(before, LANES)]
         )
-    pl.semaphore_wait(barrier, n_sec + n_gx - 2)
-
-    moves = []
+    pl.semaphore_wait(barrier, n_sec * n_gx - 1)
+
+    swaps = []
     for f, (src, dst) in enumerate(((start_ref, head), (kind_mine, kind))):
+        moves = []
+        swaps.append(moves)
         copy = pltpu.make_async_copy(
             src.at[:, :, at(here)], dst.at[layers_of(sec), 0:rows, 0:cols], own_sem.at[f]
         )
@@ -144,17 +158,15 @@
             )
             copy.start()
             moves.append(copy)
-    for copy in moves:
-        copy.wait()
 
     def packed(field, low):
-        outs = jnp.zeros((rows, LANES), f32)
+        outs = jnp.zeros((ext_r, LANES), f32)
         for l in range(total):
             if low:
-                tile = field[1 + l, 0:rows, 0:LANES]
+                tile = field[1 + l, :, 0:LANES]
                 shift = RIM * l
             else:
-                tile = field[1 + l, 0:rows, cols - LANES:cols]
+                tile = field[1 + l, :, cols - LANES:cols]
                 shift = (RIM * l + RIM) % LANES
             moved = pltpu.roll(tile, shift, 1) if shift else tile
             outs = jnp.where(lane // RIM == l, moved, outs)
@@ -194,14 +206,14 @@
             a, b = (-RIM * l) % LANES, (LANES - RIM - RIM * l) % LANES
             ra = pltpu.roll(right, a, 1) if a else right
             rb = pltpu.roll(left, b, 1) if b else left
-            field[1 + l, 0:rows, cols:] = jnp.where(lane < RIM, ra, jnp.where(lane >= LANES - RIM, rb, 0.0))
-
-    def row_copy(slot, field, first, count, d):
+            field[1 + l, :, cols:] = jnp.where(lane < RIM, ra, jnp.where(lane >= LANES - RIM, rb, 0.0))
+
+    def row_copy(slot, field, first, count, width, d):
         src = pl.ds(0, RIM) if d == 0 else pl.ds(rows - RIM, RIM)
         dst = pl.ds(rows, RIM) if d == 0 else pl.ds(rows + RIM, RIM)
         return pltpu.make_async_remote_copy(
-            src_ref=field.at[pl.ds(first, count), src, :],
-            dst_ref=field.at[pl.ds(first, count), dst, :],
+            src_ref=field.at[pl.ds(first, count), src, 0:width],
+            dst_ref=field.at[pl.ds(first, count), dst, 0:width],
             send_sem=row_send.at[slot, d],
             recv_sem=row_recv.at[slot, d],
             device_id={"gx": lax.rem(gx + n_gx - 1, n_gx) if d == 0 else lax.rem(gx + 1, n_gx)},
@@ -242,18 +254,21 @@
     none = jnp.zeros((RIM, LANES), f32)
     basis = (t0, t1, t2, t3)
 
+    outgoing = []
     for c in range(steps):
-        send_cols(c, head)
         if c == 0:
+            fields = ((0, head, 1, total, cols), (1, kind, 1, total, cols), (2, rainx, 0, steps, ext_c))
+            for f in range(2):
+                for copy in swaps[f]:
+                    copy.wait()
+                send_rows(*fields[f])
+            send_rows(*fields[2])
+            take_rows(*fields[0])
+            send_cols(c, head)
+            take_rows(*fields[1])
             send_cols(steps, kind)
-            send_rows(steps + 1, rainx, 0, steps)
-        take_cols(c, head)
-        send_rows(c, head, 1, total)
-        if c == 0:
+            take_rows(*fields[2])
             take_cols(steps, kind)
-            send_rows(steps, kind, 1, total)
-            take_rows(steps + 1, rainx, 0, steps)
-            take_rows(steps, kind, 1, total)
 
             def look(l, carry):
                 here_kind = kind[l]
@@ -268,7 +283,9 @@
                 return carry
 
             lax.fori_loop(1, total + 1, look, 0)
-        take_rows(c, head, 1, total)
+        else:
+            send_cols(c, head)
+        take_cols(c, head)
 
         def soil(s, carry):
             amount = jnp.zeros((ext_r, ext_c), f32)
@@ -295,6 +312,21 @@
             flows[s, c] = entering[own]
             entering = water[s] * entering + 0.5 * cond[(s + 1) * layers]
             leave[s] = entering
+        own_flow = pltpu.make_async_copy(flows.at[sec, c], flow_ref.at[0, c, :, at(here)], own_sem.at[3 + c])
+        own_flow.start()
+        late = [own_flow]
+        for k, peer in enumerate(sec_peers):
+            copy = pltpu.make_async_remote_copy(
+                src_ref=flows.at[peer, c],
+                dst_ref=flow_ref.at[0, c, :, at(here)],
+                send_sem=flow_send.at[c, k],
+                recv_sem=flow_recv.at[c, k],
+                device_id={"sec": peer},
+                device_id_type=MESH,
+            )
+            copy.start()
+            late.append(copy)
+        outgoing += late
 
         def faces(l, carry):
             k = cond[l]
@@ -328,7 +360,26 @@
                 acc = acc + folded(res * z)
             return acc
 
+        def land_copy(k, d, c=c):
+            src = pl.ds(0, RIM) if d == 0 else pl.ds(rows - RIM, RIM)
+            return pltpu.make_async_remote_copy(
+                src_ref=basis[k].at[pl.ds(1, total), src, 0:cols],
+                dst_ref=landed.at[c, k, d],
+                send_sem=land_send.at[c, k, d],
+                recv_sem=land_recv.at[c, k, d],
+                device_id={"gx": lax.rem(gx + n_gx - 1, n_gx) if d == 0 else lax.rem(gx + 1, n_gx)},
+                device_id_type=MESH,
+            )
+
+        def send_land(k):
+            if c + 1 < steps:
+                for d in (0, 1):
+                    @pl.when(gx > 0 if d == 0 else gx < n_gx - 1)
+                    def _(d=d):
+                        land_copy(k, d).start()
+
         g = [lax.fori_loop(0, n_sec, first, none)]
+        send_land(0)
         h = []
         for k in range(ITERS):
             def apply(l, acc, k=k):
@@ -352,46 +403,39 @@
             h.append(ah)
             if k + 1 < ITERS:
                 g.append(ag)
-
-        flat = [jnp.sum(v, axis=0, keepdims=True) for v in g + h]
-        stat_a[c, sec] = jnp.concatenate(flat, axis=0)
+                send_land(k + 1)
+
+        flat = jnp.concatenate([jnp.sum(v, axis=0, keepdims=True) for v in g + h], axis=0)
+        part = LANES // (2 * ITERS)
+        by = LANES // 2
+        while by >= part:
+            flat = flat + pltpu.roll(flat, by, 1)
+            by //= 2
+        which = lax.broadcasted_iota(jnp.int32, flat.shape, 0)
+        group = lax.broadcasted_iota(jnp.int32, flat.shape, 1) // part
+        mine = sec * n_gx + gx
+        stats[c, mine] = jnp.sum(jnp.where(which == group, flat, 0.0), axis=0, keepdims=True)
         sends = []
-        for k, peer in enumerate(sec_peers):
+        for k, peer in enumerate(everyone):
             copy = pltpu.make_async_remote_copy(
-                src_ref=stat_a.at[c, sec],
-                dst_ref=stat_a.at[c, sec],
-                send_sem=a_send.at[c, k],
-                recv_sem=a_recv.at[c, k],
-                device_id={"sec": peer},
+                src_ref=stats.at[c, mine],
+                dst_ref=stats.at[c, mine],
+                send_sem=sum_send.at[c, k],
+                recv_sem=sum_recv.at[c, k],
+                device_id=peer,
                 device_id_type=MESH,
             )
             copy.start()
             sends.append(copy)
         for copy in sends:
             copy.wait()
-        summed = stat_a[c, 0]
-        for k in range(1, n_sec):
-            summed = summed + stat_a[c, k]
-        stat_b[c, gx] = summed
-        sends = []
-        for k, peer in enumerate(gx_peers):
-            copy = pltpu.make_async_remote_copy(
-                src_ref=stat_b.at[c, gx],
-                dst_ref=stat_b.at[c, gx],
-                send_sem=b_send.at[c, k],
-                recv_sem=b_recv.at[c, k],
-                device_id={"gx": peer},
-                device_id_type=MESH,
-            )
-            copy.start()
-            sends.append(copy)
-        for copy in sends:
-            copy.wait()
-        summed = stat_b[c, 0]
-        for k in range(1, n_gx):
-            summed = summed + stat_b[c, k]
-        sums = jnp.sum(summed, axis=1, keepdims=True)
-        parts = [sums[k:k + 1] for k in range(2 * ITERS)]
+        summed = stats[c, 0]
+        for k in range(1, n_sec * n_gx):
+            summed = summed + stats[c, k]
+        parts = [
+            jnp.sum(jnp.where(group[0:1] == k, summed, 0.0), axis=1, keepdims=True)
+            for k in range(2 * ITERS)
+        ]
         x = coefficients(parts[:ITERS], parts[ITERS:])
         x = [jnp.broadcast_to(v, (rows, cols)) for v in x]
 
@@ -403,28 +447,44 @@
             return carry
 
         lax.fori_loop(1, total + 1, update, 0)
-
-    moves = []
-    for f in range(2):
-        def src(s):
-            return head.at[layers_of(s), 0:rows, 0:cols] if f == 0 else flows.at[s]
-
-        dst = out_ref.at[:, :, at(here)] if f == 0 else flow_ref.at[0, :, :, at(here)]
-        copy = pltpu.make_async_copy(src(sec), dst, own_sem.at[2 + f])
+        if c + 1 < steps:
+            for d in (0, 1):
+                @pl.when(gx > 0 if d == 0 else gx < n_gx - 1)
+                def _(d=d):
+                    for k in range(ITERS):
+                        land_copy(k, d).wait_send()
+
+                @pl.when(gx < n_gx - 1 if d == 0 else gx > 0)
+                def _(d=d):
+                    for k in range(ITERS):
+                        land_copy(k, d).wait_recv()
+
+            def update_rim(l, carry):
+                for d in (0, 1):
+                    at_rows = slice(rows + d * RIM, rows + d * RIM + RIM)
+                    v = head[l, at_rows, 0:cols]
+                    for k in range(ITERS):
+                        v = v + x[k][0:RIM] * landed[c, k, d, l - 1]
+                    head[l, at_rows, 0:cols] = v
+                return carry
+
+            lax.fori_loop(1, total + 1, update_rim, 0)
+
+    copy = pltpu.make_async_copy(head.at[layers_of(sec), 0:rows, 0:cols], out_ref.at[:, :, at(here)], own_sem.at[2])
+    copy.start()
+    outgoing.append(copy)
+    for k, peer in enumerate(sec_peers):
+        copy = pltpu.make_async_remote_copy(
+            src_ref=head.at[layers_of(peer), 0:rows, 0:cols],
+            dst_ref=out_ref.at[:, :, at(here)],
+            send_sem=back_send.at[k],
+            recv_sem=back_recv.at[k],
+            device_id={"sec": peer},
+            device_id_type=MESH,
+        )
         copy.start()
-        moves.append(copy)
-        for k, peer in enumerate(sec_peers):
-            copy = pltpu.make_async_remote_copy(
-                src_ref=src(peer),
-                dst_ref=dst,
-                send_sem=back_send.at[f, k],
-                recv_sem=back_recv.at[f, k],
-                device_id={"sec": peer},
-                device_id_type=MESH,
-            )
-            copy.start()
-            moves.append(copy)
-    for copy in moves:
+        outgoing.append(copy)
+    for copy in outgoing:
         copy.wait()
 
 
@@ -455,23 +515,25 @@
         + [
             pltpu.VMEM((steps,) + ext, f32),
             pltpu.VMEM((n_sec, steps, rows, cols), f32),
-            pltpu.VMEM((steps + 1, 2, rows, LANES), f32),
-            pltpu.VMEM((steps + 1, 2, rows, LANES), f32),
-            pltpu.VMEM((steps, n_sec, 2 * ITERS, LANES), f32),
-            pltpu.VMEM((steps, n_gx, 2 * ITERS, LANES), f32),
-            dma((4,)),
+            pltpu.VMEM((steps + 1, 2, ext[0], LANES), f32),
+            pltpu.VMEM((steps + 1, 2, ext[0], LANES), f32),
+            pltpu.VMEM((steps, ITERS, 2, total, RIM, cols), f32),
+            pltpu.VMEM((steps, n_sec * n_gx, 1, LANES), f32),
+            dma((3 + steps,)),
             dma((2, n_sec - 1)),
             dma((2, n_sec - 1)),
             dma((steps + 1, 2)),
             dma((steps + 1, 2)),
-            dma((steps + 2, 2)),
-            dma((steps + 2, 2)),
+            dma((3, 2)),
+            dma((3, 2)),
+            dma((steps, ITERS, 2)),
+            dma((steps, ITERS, 2)),
+            dma((steps, n_sec * n_gx)),
+            dma((steps, n_sec * n_gx)),
             dma((steps, n_sec - 1)),
             dma((steps, n_sec - 1)),
-            dma((steps, n_gx - 1)),
-            dma((steps, n_gx - 1)),
-            dma((2, n_sec - 1)),
-            dma((2, n_sec - 1)),
+            dma((n_sec - 1,)),
+            dma((n_sec - 1,)),
         ],
         compiler_params=pltpu.CompilerParams(collective_id=0, has_side_effects=True),
     )(start, soil, conductivity, storage, rain))

time: 96.3 us -> 83.7 us (0.87)
  Pallas kernels: 93.1 us -> 80.5 us
    pallas_call x1, Pallas kernels: 93.1 us -> 80.5 us  [body(): pl.pallas_call(functools.partial(kernel, n_sec, n_gx, steps, conductivity...]
where the time goes in v2:
time: 83.7 us; the launch traced here: 83.6 us
  Pallas kernels  80.5 us (96%)
  local copies, waits for them, and re-layouts  2.39 us (3%)
    pallas_call x1, Pallas kernels, body(): pl.pallas_call(functools.partial(kernel, n_sec, n_gx, steps, conductivity...  80.5 us
    unnamed x4, local copies, waits for them, and re-layouts  2.39 us

profile of v2, /device:TPU:0, one launch (start us, length us, event | category | flops | bytes accessed | tf_op | source)
XLA Modules:
  0.0 83.6 jit_solution(9264823387753054741)
XLA Ops:
  0.6 80.5 %shard_map.68 = (f32[4,16,1024]{2,1,0:T(8,128)}, f32[1,3,16,1024]{3,2,1,0:T(8,128)}) custom-call(f32[4,16,1024]{2,1,0:T(8,128)} %start_ref.1, s32[4,16,1024]{2,1,0:T(8,128)} %soil_ref.1, f32[12]{0:T(128)} %cond_ref.1, f32[12]{0:T(128)} %store_ref.1, f32[3,16,1024]{2,1,0:T(8,128)} %rain_ref.1), custom_call_target="tpu_custom_call" | custom-call | tf_op jit(solution)/shard_map/pallas_call | solution.py:504
  81.2 0.0 copy-start
  81.2 1.7 %copy.9 = f32[4,16,1024]{2,1,0:T(8,128)} copy(f32[4,16,1024]{2,1,0:T(8,128)} %get-tuple-element.4) | data formatting | bytes 524288
  82.9 0.0 copy-done
  82.9 0.7 copy.10
Async XLA Ops:
  81.2 1.7 %copy-start = (f32[1,3,16,1024]{3,2,1,0:T(8,128)S(1)}, f32[1,3,16,1024]{3,2,1,0:T(8,128)}, u32[]{:S(2)}) copy-start(f32[1,3,16,1024]{3,2,1,0:T(8,128)} %get-tuple-element.5) | copy-start | bytes 589828

commit v3 on v2

--- a/solution.py
+++ b/solution.py
@@ -72,9 +72,9 @@
     n_sec, n_gx, steps, kinds,
     start_ref, soil_ref, cond_ref, store_ref, rain_ref,
     out_ref, flow_ref,
-    kind_mine, head, kind, store, cond, cap, face_l, face_r, face_c, diag, dinv, t0, t1, t2, t3,
-    water, enter, leave, rainx, flows, pack_out, pack_in, landed, stats,
-    own_sem, swap_send, swap_recv, col_send, col_recv, row_send, row_recv, land_send, land_recv,
+    head, soils, kind, store, cond, cap, face_l, face_r, face_c, diag, dinv, t0, t1, t2, t3,
+    water, enter, leave, rainx, flows, pack_out, pack_in, soil_out, soil_in, landed, stats,
+    met_sem, own_sem, swap_send, swap_recv, col_send, col_recv, row_send, row_recv, land_send, land_recv,
     sum_send, sum_recv, flow_send, flow_recv, back_send, back_recv,
 ):
     f32 = jnp.float32
@@ -92,41 +92,52 @@
     def layers_of(s):
         return pl.ds(1 + s * layers, layers)
 
-    plane = jnp.zeros((ext_r, ext_c), f32)
-    for ref in (head, kind, cond, t0, t1, t2, t3, face_l):
-        ref[0] = plane
-        ref[total + 1] = plane
-
-    def clear(l, carry):
-        for ref in (head, kind):
-            ref[l, rows:, :] = jnp.zeros((2 * RIM, ext_c), f32)
-        return carry
-
-    lax.fori_loop(1, total + 1, clear, 0)
-    for c in range(steps):
-        rainx[c] = plane
-    pack_in[...] = jnp.zeros_like(pack_in)
-    kind_mine[...] = soil_ref[...].astype(f32) + 1.0
-
-    @pl.when(jnp.logical_or(gx == 0, gx == n_gx - 1))
-    def _():
-        def wipe(l, carry):
-            for c in range(steps - 1):
-                for k in range(ITERS):
-                    for d in (0, 1):
-                        landed[c, k, d, l] = jnp.zeros((RIM, cols), f32)
-            return carry
-
-        lax.fori_loop(0, total, wipe, 0)
-
     sec_peers = [lax.rem(sec + k, n_sec) for k in range(1, n_sec)]
+    gx_peers = [lax.rem(gx + k, n_gx) for k in range(1, n_gx)]
     everyone = [
         {"sec": lax.rem(sec + i, n_sec), "gx": lax.rem(gx + j, n_gx)}
         for j in range(n_gx) for i in range(n_sec) if i + j
     ]
     barrier = pltpu.get_barrier_semaphore()
-    for peer in everyone:
-        pl.semaphore_signal(barrier, inc=1, device_id=peer, device_id_type=MESH)
+    for peer in sec_peers:
+        pl.semaphore_signal(barrier, inc=1, device_id={"sec": peer}, device_id_type=MESH)
+    for peer in gx_peers:
+        pl.semaphore_signal(barrier, inc=1, device_id={"gx": peer}, device_id_type=MESH)
+
+    plane = jnp.zeros((ext_r, ext_c), f32)
+    for ref in (head, cond, t0, t1, t2, t3, face_l):
+        ref[0] = plane
+        ref[total + 1] = plane
+    for d in (0, 1):
+        rim = slice(rows + d * RIM, rows + d * RIM + RIM)
+
+        @pl.when(gx == n_gx - 1 if d == 0 else gx == 0)
+        def _(d=d, rim=rim):
+            def wipe(l, carry):
+                head[l + 1, rim, :] = jnp.zeros((RIM, ext_c), f32)
+                soils[l + 1, rim, :] = jnp.zeros((RIM, ext_c), jnp.int32)
+                for c in range(steps - 1):
+                    for k in range(ITERS):
+                        landed[c, k, d, l] = jnp.zeros((RIM, cols), f32)
+                return carry
+
+            lax.fori_loop(0, total, wipe, 0)
+            for c in range(steps):
+                rainx[c, rim, :] = jnp.zeros((RIM, ext_c), f32)
+
+        @pl.when(here == n_sec - 1 if d == 0 else here == 0)
+        def _(d=d):
+            for c in range(steps):
+                pack_in[c, d] = jnp.zeros((ext_r, LANES), f32)
+            soil_in[d] = jnp.zeros((ext_r, LANES), jnp.int32)
+
+    at_row = lax.broadcasted_iota(jnp.int32, (ext_r, ext_c), 0)
+    at_col = lax.broadcasted_iota(jnp.int32, (ext_r, ext_c), 1)
+    outside = (at_col >= cols + RIM) & (at_col < ext_c - RIM)
+    outside = outside | ((at_row >= rows) & (at_row < rows + RIM) & (gx == n_gx - 1))
+    outside = outside | ((at_row >= rows + RIM) & (gx == 0))
+    outside = outside | ((at_col >= cols) & (at_col < cols + RIM) & (here == n_sec - 1))
+    outside = outside | ((at_col >= ext_c - RIM) & (here == 0))
 
     lane = lax.broadcasted_iota(jnp.int32, (ext_r, LANES), 1)
     after = pl.multiple_of(lax.rem(here + 1, n_sec) * cols, LANES)
@@ -136,10 +147,12 @@
         rainx[c, 0:rows, cols:] = jnp.where(
             lane[0:rows] < LANES // 2, rain_ref[c, :, pl.ds(after, LANES)], rain_ref[c, :, pl.ds(before, LANES)]
         )
-    pl.semaphore_wait(barrier, n_sec * n_gx - 1)
+    pl.semaphore_wait(barrier, n_sec + n_gx - 2)
+    for peer in sec_peers:
+        pl.semaphore_signal(met_sem, inc=1, device_id={"sec": peer}, device_id_type=MESH)
 
     swaps = []
-    for f, (src, dst) in enumerate(((start_ref, head), (kind_mine, kind))):
+    for f, (src, dst) in enumerate(((start_ref, head), (soil_ref, soils))):
         moves = []
         swaps.append(moves)
         copy = pltpu.make_async_copy(
@@ -160,7 +173,7 @@
             moves.append(copy)
 
     def packed(field, low):
-        outs = jnp.zeros((ext_r, LANES), f32)
+        outs = jnp.zeros((ext_r, LANES), field.dtype)
         for l in range(total):
             if low:
                 tile = field[1 + l, :, 0:LANES]
@@ -173,17 +186,21 @@
         return outs
 
     def send_cols(slot, field):
-        pack_out[slot, 0] = packed(field, True)
-        pack_out[slot, 1] = packed(field, False)
+        out, _ = packs(slot)
+        out[0] = packed(field, True)
+        out[1] = packed(field, False)
         for d in (0, 1):
             @pl.when(here > 0 if d == 0 else here < n_sec - 1)
             def _(d=d):
                 col_copy(slot, d).start()
 
+    def packs(slot):
+        return (pack_out.at[slot], pack_in.at[slot]) if slot < steps else (soil_out, soil_in)
+
     def col_copy(slot, d):
         return pltpu.make_async_remote_copy(
-            src_ref=pack_out.at[slot, d],
-            dst_ref=pack_in.at[slot, d],
+            src_ref=packs(slot)[0].at[d],
+            dst_ref=packs(slot)[1].at[d],
             send_sem=col_send.at[slot, d],
             recv_sem=col_recv.at[slot, d],
             device_id={"sec": place_of(lax.rem(here + n_sec - 1, n_sec) if d == 0 else lax.rem(here + 1, n_sec))},
@@ -201,12 +218,13 @@
             col_copy(slot, 1).wait_send()
             col_copy(slot, 0).wait_recv()
 
-        right, left = pack_in[slot, 0], pack_in[slot, 1]
+        taken = packs(slot)[1]
+        right, left, nil = taken[0], taken[1], jnp.zeros((ext_r, LANES), field.dtype)
         for l in range(total):
             a, b = (-RIM * l) % LANES, (LANES - RIM - RIM * l) % LANES
             ra = pltpu.roll(right, a, 1) if a else right
             rb = pltpu.roll(left, b, 1) if b else left
-            field[1 + l, :, cols:] = jnp.where(lane < RIM, ra, jnp.where(lane >= LANES - RIM, rb, 0.0))
+            field[1 + l, :, cols:] = jnp.where(lane < RIM, ra, jnp.where(lane >= LANES - RIM, rb, nil))
 
     def row_copy(slot, field, first, count, width, d):
         src = pl.ds(0, RIM) if d == 0 else pl.ds(rows - RIM, RIM)
@@ -257,7 +275,7 @@
     outgoing = []
     for c in range(steps):
         if c == 0:
-            fields = ((0, head, 1, total, cols), (1, kind, 1, total, cols), (2, rainx, 0, steps, ext_c))
+            fields = ((0, head, 1, total, cols), (1, soils, 1, total, cols), (2, rainx, 0, steps, ext_c))
             for f in range(2):
                 for copy in swaps[f]:
                     copy.wait()
@@ -266,20 +284,25 @@
             take_rows(*fields[0])
             send_cols(c, head)
             take_rows(*fields[1])
-            send_cols(steps, kind)
+            send_cols(steps, soils)
             take_rows(*fields[2])
-            take_cols(steps, kind)
+            take_cols(steps, soils)
+
+            spot = lax.broadcasted_iota(jnp.int32, (ext_r, LANES), 1)
+            of_cond = jnp.zeros((ext_r, LANES), f32)
+            of_store = jnp.zeros((ext_r, LANES), f32)
+            for k in range(kinds):
+                of_cond = jnp.where(spot == k, cond_ref[k], of_cond)
+                of_store = jnp.where(spot == k, store_ref[k], of_store)
 
             def look(l, carry):
-                here_kind = kind[l]
-                a = jnp.zeros((ext_r, ext_c), f32)
-                b = jnp.zeros((ext_r, ext_c), f32)
-                for k in range(kinds):
-                    same = here_kind == jnp.float32(k + 1)
-                    a = jnp.where(same, cond_ref[k], a)
-                    b = jnp.where(same, store_ref[k], b)
-                kind[l] = a
-                store[l] = b
+                for j in range(0, ext_c, LANES):
+                    which = soils[l, :, j:j + LANES]
+                    hide = outside[:, j:j + LANES]
+                    a = jnp.take_along_axis(of_cond, which, axis=1, mode="promise_in_bounds")
+                    b = jnp.take_along_axis(of_store, which, axis=1, mode="promise_in_bounds")
+                    kind[l, :, j:j + LANES] = jnp.where(hide, 0.0, a)
+                    store[l, :, j:j + LANES] = jnp.where(hide, 0.0, b)
                 return carry
 
             lax.fori_loop(1, total + 1, look, 0)
@@ -415,6 +438,8 @@
         group = lax.broadcasted_iota(jnp.int32, flat.shape, 1) // part
         mine = sec * n_gx + gx
         stats[c, mine] = jnp.sum(jnp.where(which == group, flat, 0.0), axis=0, keepdims=True)
+        if c == 0:
+            pl.semaphore_wait(met_sem, n_sec - 1)
         sends = []
         for k, peer in enumerate(everyone):
             copy = pltpu.make_async_remote_copy(
@@ -500,6 +525,7 @@
     per_sec = pltpu.VMEM((n_sec,) + ext, f32)
     dma = pltpu.SemaphoreType.DMA
     vmem = pl.BlockSpec(memory_space=pltpu.VMEM)
+    hbm = pl.BlockSpec(memory_space=pl.ANY)
     smem = pl.BlockSpec(memory_space=pltpu.SMEM)
     return tuple(pl.pallas_call(
         functools.partial(kernel, n_sec, n_gx, steps, conductivity.shape[0]),
@@ -507,18 +533,21 @@
             jax.ShapeDtypeStruct(start.shape, f32),
             jax.ShapeDtypeStruct((1, steps, rows, wide), f32),
         ),
-        in_specs=[vmem, vmem, smem, smem, vmem],
-        out_specs=(vmem, vmem),
-        scratch_shapes=[pltpu.VMEM(start.shape, f32)]
-        + [field] * 14
+        in_specs=[hbm, hbm, smem, smem, vmem],
+        out_specs=(hbm, hbm),
+        scratch_shapes=[field, pltpu.VMEM((total + 2,) + ext, jnp.int32)]
+        + [field] * 13
         + [per_sec] * 3
         + [
             pltpu.VMEM((steps,) + ext, f32),
             pltpu.VMEM((n_sec, steps, rows, cols), f32),
-            pltpu.VMEM((steps + 1, 2, ext[0], LANES), f32),
-            pltpu.VMEM((steps + 1, 2, ext[0], LANES), f32),
+            pltpu.VMEM((steps, 2, ext[0], LANES), f32),
+            pltpu.VMEM((steps, 2, ext[0], LANES), f32),
+            pltpu.VMEM((2, ext[0], LANES), jnp.int32),
+            pltpu.VMEM((2, ext[0], LANES), jnp.int32),
             pltpu.VMEM((steps, ITERS, 2, total, RIM, cols), f32),
             pltpu.VMEM((steps, n_sec * n_gx, 1, LANES), f32),
+            pltpu.SemaphoreType.REGULAR,
             dma((3 + steps,)),
             dma((2, n_sec - 1)),
             dma((2, n_sec - 1)),

time: 83.7 us -> 82.1 us (0.981)
  Pallas kernels: 80.5 us -> 78.9 us
    pallas_call x1, Pallas kernels: 80.5 us -> 78.9 us  [body(): pl.pallas_call(functools.partial(kernel, n_sec, n_gx, steps, conductivity...]
where the time goes in v3:
time: 82.1 us; the launch traced here: 81.9 us
  Pallas kernels  78.9 us (96%)
  local copies, waits for them, and re-layouts  2.39 us (3%)
    pallas_call x1, Pallas kernels, body(): pl.pallas_call(functools.partial(kernel, n_sec, n_gx, steps, conductivity...  78.9 us
    unnamed x4, local copies, waits for them, and re-layouts  2.39 us

profile of v3, /device:TPU:0, one launch (start us, length us, event | category | flops | bytes accessed | tf_op | source)
XLA Modules:
  0.0 81.9 jit_solution(1891288320676324714)
XLA Ops:
  0.6 78.9 %shard_map.68 = (f32[4,16,1024]{2,1,0:T(8,128)}, f32[1,3,16,1024]{3,2,1,0:T(8,128)}) custom-call(f32[4,16,1024]{2,1,0:T(8,128)} %start_ref.1, s32[4,16,1024]{2,1,0:T(8,128)} %soil_ref.1, f32[12]{0:T(128)} %cond_ref.1, f32[12]{0:T(128)} %store_ref.1, f32[3,16,1024]{2,1,0:T(8,128)} %rain_ref.1), custom_call_target="tpu_custom_call" | custom-call | tf_op jit(solution)/shard_map/pallas_call | solution.py:530
  79.5 0.0 copy-start
  79.5 1.7 %copy.9 = f32[4,16,1024]{2,1,0:T(8,128)} copy(f32[4,16,1024]{2,1,0:T(8,128)} %get-tuple-element.4) | data formatting | bytes 524288
  81.2 0.0 copy-done
  81.3 0.7 copy.10
Async XLA Ops:
  79.5 1.7 %copy-start = (f32[1,3,16,1024]{3,2,1,0:T(8,128)S(1)}, f32[1,3,16,1024]{3,2,1,0:T(8,128)}, u32[]{:S(2)}) copy-start(f32[1,3,16,1024]{3,2,1,0:T(8,128)} %get-tuple-element.5) | copy-start | bytes 589828

commit v4 on v3

--- a/solution.py
+++ b/solution.py
@@ -272,6 +272,16 @@
     none = jnp.zeros((RIM, LANES), f32)
     basis = (t0, t1, t2, t3)
 
+    def back_copy(k, peer):
+        return pltpu.make_async_remote_copy(
+            src_ref=head.at[layers_of(peer), 0:rows, 0:cols],
+            dst_ref=out_ref.at[:, :, at(here)],
+            send_sem=back_send.at[k],
+            recv_sem=back_recv.at[k],
+            device_id={"sec": peer},
+            device_id_type=MESH,
+        )
+
     outgoing = []
     for c in range(steps):
         if c == 0:
@@ -286,7 +296,6 @@
             take_rows(*fields[1])
             send_cols(steps, soils)
             take_rows(*fields[2])
-            take_cols(steps, soils)
 
             spot = lax.broadcasted_iota(jnp.int32, (ext_r, LANES), 1)
             of_cond = jnp.zeros((ext_r, LANES), f32)
@@ -295,8 +304,8 @@
                 of_cond = jnp.where(spot == k, cond_ref[k], of_cond)
                 of_store = jnp.where(spot == k, store_ref[k], of_store)
 
-            def look(l, carry):
-                for j in range(0, ext_c, LANES):
+            def look(lanes, l, carry):
+                for j in range(lanes.start, lanes.stop, LANES):
                     which = soils[l, :, j:j + LANES]
                     hide = outside[:, j:j + LANES]
                     a = jnp.take_along_axis(of_cond, which, axis=1, mode="promise_in_bounds")
@@ -305,36 +314,55 @@
                     store[l, :, j:j + LANES] = jnp.where(hide, 0.0, b)
                 return carry
 
-            lax.fori_loop(1, total + 1, look, 0)
         else:
             send_cols(c, head)
-        take_cols(c, head)
-
-        def soil(s, carry):
-            amount = jnp.zeros((ext_r, ext_c), f32)
+
+        def soil(lanes, s, carry):
+            amount = jnp.zeros((ext_r, lanes.stop - lanes.start), f32)
             for j in range(layers):
                 l = 1 + s * layers + j
-                sat = jax.nn.sigmoid(head[l])
-                cond[l] = kind[l] * (0.05 + sat * sat)
-                cap[l] = store[l] * (0.1 + sat * (1.0 - sat))
+                sat = jax.nn.sigmoid(head[l, :, lanes])
+                cond[l, :, lanes] = kind[l, :, lanes] * (0.05 + sat * sat)
+                cap[l, :, lanes] = store[l, :, lanes] * (0.1 + sat * (1.0 - sat))
                 amount = amount + sat
-            water[s] = amount
+            water[s, :, lanes] = amount
             return carry
 
-        lax.fori_loop(0, n_sec, soil, 0)
-
-        depth = jnp.float32(layers)
-        below = jnp.zeros((ext_r, ext_c), f32)
-        for s in reversed(range(n_sec)):
-            amount = water[s]
-            water[s] = amount / depth * (0.5 + 0.5 * below / (below + depth))
-            below = below + amount
-        entering = rainx[c]
-        for s in range(n_sec):
-            enter[s] = entering
-            flows[s, c] = entering[own]
-            entering = water[s] * entering + 0.5 * cond[(s + 1) * layers]
-            leave[s] = entering
+        def couple(lanes):
+            depth = jnp.float32(layers)
+            below = jnp.zeros((ext_r, lanes.stop - lanes.start), f32)
+            slopes = [None] * n_sec
+            for s in reversed(range(n_sec)):
+                amount = water[s, :, lanes]
+                slopes[s] = amount / depth * (0.5 + 0.5 * below / (below + depth))
+                below = below + amount
+            entering = rainx[c, :, lanes]
+            for s in range(n_sec):
+                enter[s, :, lanes] = entering
+                if lanes.start == 0:
+                    flows[s, c] = entering[own]
+                entering = slopes[s] * entering + 0.5 * cond[(s + 1) * layers, :, lanes]
+                leave[s, :, lanes] = entering
+
+        def faces(lanes, l, carry):
+            k = cond[l, :, lanes]
+            face_l[l, :, lanes] = harmonic(k, cond[l + 1, :, lanes])
+            face_r[l, :, lanes] = harmonic(k, shift(k, -1, 0))
+            return carry
+
+        def faces_across(l, carry):
+            k = cond[l]
+            face_c[l] = harmonic(k, shift(k, -1, 1))
+            return carry
+
+        def prepare(lanes):
+            if c == 0:
+                lax.fori_loop(1, total + 1, functools.partial(look, lanes), 0)
+            lax.fori_loop(0, n_sec, functools.partial(soil, lanes), 0)
+            couple(lanes)
+            lax.fori_loop(1, total + 1, functools.partial(faces, lanes), 0)
+
+        prepare(slice(0, cols))
         own_flow = pltpu.make_async_copy(flows.at[sec, c], flow_ref.at[0, c, :, at(here)], own_sem.at[3 + c])
         own_flow.start()
         late = [own_flow]
@@ -351,14 +379,11 @@
             late.append(copy)
         outgoing += late
 
-        def faces(l, carry):
-            k = cond[l]
-            face_l[l] = harmonic(k, cond[l + 1])
-            face_r[l] = harmonic(k, shift(k, -1, 0))
-            face_c[l] = harmonic(k, shift(k, -1, 1))
-            return carry
-
-        lax.fori_loop(1, total + 1, faces, 0)
+        if c == 0:
+            take_cols(steps, soils)
+        take_cols(c, head)
+        prepare(slice(cols, ext_c))
+        lax.fori_loop(1, total + 1, faces_across, 0)
 
         def first(s, acc):
             for j in range(layers):
@@ -471,7 +496,15 @@
             head[l, 0:rows, 0:cols] = v
             return carry
 
-        lax.fori_loop(1, total + 1, update, 0)
+        if c + 1 == steps:
+            for i in range(1, n_sec):
+                peer = sec_peers[i - 1]
+                lax.fori_loop(1 + peer * layers, 1 + (peer + 1) * layers, update, 0)
+                back_copy(i - 1, peer).start()
+                outgoing.append(back_copy(i - 1, peer))
+            lax.fori_loop(1 + sec * layers, 1 + (sec + 1) * layers, update, 0)
+        else:
+            lax.fori_loop(1, total + 1, update, 0)
         if c + 1 < steps:
             for d in (0, 1):
                 @pl.when(gx > 0 if d == 0 else gx < n_gx - 1)
@@ -498,17 +531,6 @@
     copy = pltpu.make_async_copy(head.at[layers_of(sec), 0:rows, 0:cols], out_ref.at[:, :, at(here)], own_sem.at[2])
     copy.start()
     outgoing.append(copy)
-    for k, peer in enumerate(sec_peers):
-        copy = pltpu.make_async_remote_copy(
-            src_ref=head.at[layers_of(peer), 0:rows, 0:cols],
-            dst_ref=out_ref.at[:, :, at(here)],
-            send_sem=back_send.at[k],
-            recv_sem=back_recv.at[k],
-            device_id={"sec": peer},
-            device_id_type=MESH,
-        )
-        copy.start()
-        outgoing.append(copy)
     for copy in outgoing:
         copy.wait()
 

time: 82.1 us -> 81.5 us (level)
  no operation moved by 1% of the time
where the time goes in v4:
time: 81.5 us; the launch traced here: 81.3 us
  Pallas kernels  78.3 us (96%)
  local copies, waits for them, and re-layouts  2.39 us (3%)
    pallas_call x1, Pallas kernels, body(): pl.pallas_call(functools.partial(kernel, n_sec, n_gx, steps, conductivity...  78.3 us
    unnamed x4, local copies, waits for them, and re-layouts  2.39 us

profile of v4, /device:TPU:0, one launch (start us, length us, event | category | flops | bytes accessed | tf_op | source)
XLA Modules:
  0.0 81.3 jit_solution(3537371878336261757)
XLA Ops:
  0.6 78.3 %shard_map.68 = (f32[4,16,1024]{2,1,0:T(8,128)}, f32[1,3,16,1024]{3,2,1,0:T(8,128)}) custom-call(f32[4,16,1024]{2,1,0:T(8,128)} %start_ref.1, s32[4,16,1024]{2,1,0:T(8,128)} %soil_ref.1, f32[12]{0:T(128)} %cond_ref.1, f32[12]{0:T(128)} %store_ref.1, f32[3,16,1024]{2,1,0:T(8,128)} %rain_ref.1), custom_call_target="tpu_custom_call" | custom-call | tf_op jit(solution)/shard_map/pallas_call | solution.py:552
  78.9 0.0 copy-start
  78.9 1.7 %copy.9 = f32[4,16,1024]{2,1,0:T(8,128)} copy(f32[4,16,1024]{2,1,0:T(8,128)} %get-tuple-element.4) | data formatting | bytes 524288
  80.6 0.0 copy-done
  80.6 0.7 copy.10
Async XLA Ops:
  78.9 1.7 %copy-start = (f32[1,3,16,1024]{3,2,1,0:T(8,128)S(1)}, f32[1,3,16,1024]{3,2,1,0:T(8,128)}, u32[]{:S(2)}) copy-start(f32[1,3,16,1024]{3,2,1,0:T(8,128)} %get-tuple-element.5) | copy-start | bytes 589828

commit v5 on v4

--- a/solution.py
+++ b/solution.py
@@ -187,9 +187,9 @@
 
     def send_cols(slot, field):
         out, _ = packs(slot)
-        out[0] = packed(field, True)
-        out[1] = packed(field, False)
         for d in (0, 1):
+            out[d] = packed(field, d == 0)
+
             @pl.when(here > 0 if d == 0 else here < n_sec - 1)
             def _(d=d):
                 col_copy(slot, d).start()

time: 81.5 us -> 81.6 us (level)
  no operation moved by 1% of the time
where the time goes in v5:
time: 81.6 us; the launch traced here: 81.4 us
  Pallas kernels  78.4 us (96%)
  local copies, waits for them, and re-layouts  2.39 us (3%)
    pallas_call x1, Pallas kernels, body(): pl.pallas_call(functools.partial(kernel, n_sec, n_gx, steps, conductivity...  78.4 us
    unnamed x4, local copies, waits for them, and re-layouts  2.39 us

profile of v5, /device:TPU:0, one launch (start us, length us, event | category | flops | bytes accessed | tf_op | source)
XLA Modules:
  0.0 81.4 jit_solution(11027226065160369073)
XLA Ops:
  0.6 78.4 %shard_map.68 = (f32[4,16,1024]{2,1,0:T(8,128)}, f32[1,3,16,1024]{3,2,1,0:T(8,128)}) custom-call(f32[4,16,1024]{2,1,0:T(8,128)} %start_ref.1, s32[4,16,1024]{2,1,0:T(8,128)} %soil_ref.1, f32[12]{0:T(128)} %cond_ref.1, f32[12]{0:T(128)} %store_ref.1, f32[3,16,1024]{2,1,0:T(8,128)} %rain_ref.1), custom_call_target="tpu_custom_call" | custom-call | tf_op jit(solution)/shard_map/pallas_call | solution.py:552
  79.0 0.0 copy-start
  79.0 1.7 %copy.9 = f32[4,16,1024]{2,1,0:T(8,128)} copy(f32[4,16,1024]{2,1,0:T(8,128)} %get-tuple-element.4) | data formatting | bytes 524288
  80.7 0.0 copy-done
  80.7 0.7 copy.10
Async XLA Ops:
  79.0 1.7 %copy-start = (f32[1,3,16,1024]{3,2,1,0:T(8,128)S(1)}, f32[1,3,16,1024]{3,2,1,0:T(8,128)}, u32[]{:S(2)}) copy-start(f32[1,3,16,1024]{3,2,1,0:T(8,128)} %get-tuple-element.5) | copy-start | bytes 589828
